TPU v7x, 512 devices: a whole 4x4x16 slice. The times are simulated.
512 devices in a mesh: slab: 64 (over z, x_hi, core), band: 8 (over y, x_lo).
Axes of the slice: x: 4 (x_hi: 2, x_lo: 2; x = x_hi * 2 + x_lo), y: 4, z: 16, core: 2. Of those that a mesh axis runs over, the one named last changes fastest.
Arguments:
- hamiltonian: bfloat16 [512, 7, 128, 128], P('slab', None, 'band'), may hold values from -0.1875 to 0.1875
- neighbors: int32 [512, 7], P('slab'), may hold values from 0 to 11, as said below
- orbitals: bfloat16 [65536, 1024], P('slab', 'band'), may hold values from -6 to 6
Outputs:
- residual: bfloat16 [65536, 1024], P(('slab', 'band'))
Inputs may be any that keep to these rules, and one draw needn't show every extreme that they name: `neighbors`: window positions 0 to 1 are the last 2 elements of the slab below (periodic), 2 to 9 the slab's own elements, the rest the first 2 elements of the slab above. A slab's elements are in layers of 2; each block row names, in an order of its own, itself, the element 2 positions below and above it in the window, and four elements of its own layer (repeats possible).
All inputs are finite; a program needn't handle non-finite values.
Results may differ from a plain program's by a relative error of at most 0.012.
Values may be sent and summed in bfloat16 or wider, within the bound.
No kernel may reach another device: no remote copies, remote signals or barrier semaphores. Data moves between devices by JAX's collectives and lax.ppermute only.
A program may use at most 64 MiB of HBM per device.

v0:
```python
import math
import jax
import jax.numpy as jnp
from jax import lax
from jax.sharding import PartitionSpec as P

FACE = 2


def padded(block, sides, width):
    for axis, dim in sides:
        count = lax.axis_size(axis)
        forward = [(i, i + 1) for i in range(count - 1)]
        forward.append((count - 1, 0))
        backward = [(target, source) for source, target in forward]
        low = lax.ppermute(
            lax.slice_in_dim(block, block.shape[dim] - width, None, axis=dim), axis, forward
        )
        high = lax.ppermute(lax.slice_in_dim(block, 0, width, axis=dim), axis, backward)
        block = jnp.concatenate([low, block, high], axis=dim)
    return block


def apply_local(vector, full_tiles, neighbors):
    tile_size = full_tiles.shape[2]
    extended = padded(vector, (("slab", 0),), FACE * tile_size)
    blocks = extended.reshape(-1, tile_size, vector.shape[1])
    picked_blocks = blocks[neighbors]
    product = jnp.einsum(
        "rjab,rjbc->rac", full_tiles, picked_blocks, preferred_element_type=jnp.float32
    )
    return product.reshape(vector.shape[0], vector.shape[1])


def body(hamiltonian, neighbors, orbitals):
    full_tiles = lax.all_gather(hamiltonian, "band", axis=2, tiled=True)
    first = apply_local(orbitals, full_tiles, neighbors).astype(jnp.bfloat16)
    second = (
        2.0 * apply_local(first, full_tiles, neighbors) - orbitals.astype(jnp.float32)
    ).astype(jnp.bfloat16)
    third = (2.0 * apply_local(second, full_tiles, neighbors) - first.astype(jnp.float32)).astype(
        jnp.bfloat16
    )
    applied = apply_local(third, full_tiles, neighbors).astype(jnp.bfloat16)
    rows_all = orbitals.shape[0] * lax.axis_size("slab")
    bands_all = orbitals.shape[1] * lax.axis_size("band")
    gram_scale = 1.0 / math.sqrt(float(rows_all) * float(bands_all))
    strip_third, strip_applied = (
        lax.all_to_all(third, "band", split_axis=0, concat_axis=1, tiled=True),
        lax.all_to_all(applied, "band", split_axis=0, concat_axis=1, tiled=True),
    )
    partial_value = jnp.einsum(
        "rb,rc->bc", strip_third, strip_applied, preferred_element_type=jnp.float32
    )
    summed = lax.psum(partial_value, ("slab", "band"))
    gram_full = (summed * gram_scale).astype(jnp.bfloat16)
    mixed = jnp.dot(strip_third, gram_full, preferred_element_type=jnp.float32)
    return (strip_applied.astype(jnp.float32) - mixed).astype(jnp.bfloat16)


def solution(mesh):
    in_specs = (P("slab", None, "band", None), P("slab", None), P("slab", "band"))
    out_specs = P(("slab", "band"), None)
    return jax.shard_map(body, mesh=mesh, in_specs=in_specs, out_specs=out_specs, check_vma=False)
```

profile of v0, /device:TPU:2, one launch (start us, length us, event | category | flops | bytes accessed | tf_op | source)
XLA Modules:
  0.0 640.3 jit_solution(16940214057220224389)
XLA Ops:
  6.5 0.0 all-gather.2.cloned.1.call-start
  6.5 0.7 all-gather.2.cloned.1.call-update
  7.3 0.9 fusion.16
  8.1 1.9 collective-permute-start
  10.1 12.4 %collective-permute-start.1 = (bf16[256,128]{1,0:T(8,128)(2,1)S(1)}, bf16[256,128]{1,0:T(8,128)(2,1)S(1)}, u32[]{:S(2)}, u32[]{:S(2)}) collective-permute-start(bf16[256,128]{1,0:T(8,128)(2,1)S(1)} %get-tuple-element.12), channel_id=1, source_target_pairs={{8,0},{16,8},{24,16},{32,24},{40,32},{48,40},{56,48},{64,56},{72,6... | collective-permute-start | bytes 196616 | tf_op jit(solution)/shard_map/ppermute | solution.py:19
  22.5 0.7 compare_select_fusion
  23.2 0.1 reshape.35
  23.3 0.0 collective-permute-done
  23.3 1.1 collective-permute-done.1
  24.4 1.0 pad_maximum_fusion
  25.3 0.9 gather_fusion
  26.3 42.6 %all-gather.2.cloned.1.call-done = bf16[8,7,128,128]{3,2,1,0:T(8,128)(2,1)} async-done(((bf16[8,7,16,128]{3,2,1,0:T(8,128)(2,1)}), bf16[8,7,128,128]{3,2,1,0:T(8,128)(2,1)}) %all-gather.2.cloned.1.call-update) | async-done | bytes 1835024 | tf_op jit(solution)/shard_map/all_gather | solution.py:36
  68.9 2.1 fusion.6
  71.0 3.2 collective-permute-start.3
  74.2 1.9 collective-permute-start.2
  76.2 0.0 collective-permute-done.3
  76.2 7.3 %collective-permute-done.2 = bf16[256,128]{1,0:T(8,128)(2,1)S(1)} collective-permute-done((bf16[256,128]{1,0:T(8,128)(2,1)S(1)}, bf16[256,128]{1,0:T(8,128)(2,1)S(1)}, u32[]{:S(2)}, u32[]{:S(2)}) %collective-permute-start.2) | collective-permute-done | bytes 65568 | tf_op jit(solution)/shard_map/ppermute | solution.py:16
  83.5 0.0 copy-start
  83.5 2.0 gather_fusion.1
  85.5 0.0 copy-done
  85.5 0.0 copy-start.1
  85.5 2.2 fusion.3
  87.7 0.0 copy-done.1
  87.7 0.1 fusion.10
  87.8 1.9 collective-permute-start.4
  89.7 7.3 %collective-permute-start.5 = (bf16[256,128]{1,0:T(8,128)(2,1)S(1)}, bf16[256,128]{1,0:T(8,128)(2,1)S(1)}, u32[]{:S(2)}, u32[]{:S(2)}) collective-permute-start(bf16[256,128]{1,0:T(8,128)(2,1)S(1)} %get-tuple-element.8), channel_id=1, source_target_pairs={{8,0},{16,8},{24,16},{32,24},{40,32},{48,40},{56,48},{64,56},{72,6... | collective-permute-start | bytes 196616 | tf_op jit(solution)/shard_map/ppermute | solution.py:19
  97.0 0.0 collective-permute-done.4
  97.0 1.9 collective-permute-done.5
  98.9 2.1 gather_fusion.2
  101.0 2.1 fusion.4
  103.1 0.1 fusion.9
  103.2 1.9 collective-permute-start.6
  105.1 7.3 %collective-permute-start.7 = (bf16[256,128]{1,0:T(8,128)(2,1)S(1)}, bf16[256,128]{1,0:T(8,128)(2,1)S(1)}, u32[]{:S(2)}, u32[]{:S(2)}) collective-permute-start(bf16[256,128]{1,0:T(8,128)(2,1)S(1)} %get-tuple-element.6), channel_id=1, source_target_pairs={{8,0},{16,8},{24,16},{32,24},{40,32},{48,40},{56,48},{64,56},{72,6... | collective-permute-start | bytes 196616 | tf_op jit(solution)/shard_map/ppermute | solution.py:19
  112.4 0.8 fusion.11
  113.2 6.0 all-to-all-start.1
  119.2 0.0 collective-permute-done.6
  119.2 0.0 collective-permute-done.7
  119.3 2.1 gather_fusion.3
  121.4 3.0 fusion.8
  124.3 1.0 all-to-all-done.1
  125.4 4.7 all-to-all-start
  130.0 0.0 all-reduce.2.cloned.1.call-start
  130.0 0.2 copy.7
  130.2 5.9 all-to-all-done
  136.2 2.7 fusion.17
  138.9 0.0 all-reduce.2.cloned.1.call-update
  138.9 0.1 copy.6
  139.0 491.1 %all-reduce.2.cloned.1.call-done = f32[1024,1024]{1,0:T(8,128)} async-done(((f32[1024,1024]{1,0:T(8,128)}), f32[1024,1024]{1,0:T(8,128)}) %all-reduce.2.cloned.1.call-update) | async-done | bytes 4194320 | tf_op jit(solution)/shard_map/psum | solution.py:55
  630.1 3.4 fusion.7
  (7 shorter events, 0.1 us)
Async XLA Ops:
  6.5 62.3 %all-gather.2.cloned.1.call-start = ((), (), s32[]{:S(2)}) async-start(), calls=%async_computation.2 | async-start | bytes 2064384 | tf_op jit(solution)/shard_map/all_gather | solution.py:36
  8.1 15.1 %collective-permute-start = (bf16[256,128]{1,0:T(8,128)(2,1)S(1)}, bf16[256,128]{1,0:T(8,128)(2,1)S(1)}, u32[]{:S(2)}, u32[]{:S(2)}) collective-permute-start(bf16[256,128]{1,0:T(8,128)(2,1)S(1)} %get-tuple-element.11), channel_id=1, source_target_pairs={{0,8},{8,16},{16,24},{24,32},{32,40},{40,48},{48,56},{56,64},{64,7... | collective-permute-start | bytes 196616 | tf_op jit(solution)/shard_map/ppermute | solution.py:16
  10.1 14.3 %collective-permute-start.1 = (bf16[256,128]{1,0:T(8,128)(2,1)S(1)}, bf16[256,128]{1,0:T(8,128)(2,1)S(1)}, u32[]{:S(2)}, u32[]{:S(2)}) collective-permute-start(bf16[256,128]{1,0:T(8,128)(2,1)S(1)} %get-tuple-element.12), channel_id=1, source_target_pairs={{8,0},{16,8},{24,16},{32,24},{40,32},{48,40},{56,48},{64,56},{72,6... | collective-permute-start | bytes 196616 | tf_op jit(solution)/shard_map/ppermute | solution.py:19
  71.0 5.2 collective-permute-start.3
  74.2 9.2 %collective-permute-start.2 = (bf16[256,128]{1,0:T(8,128)(2,1)S(1)}, bf16[256,128]{1,0:T(8,128)(2,1)S(1)}, u32[]{:S(2)}, u32[]{:S(2)}) collective-permute-start(bf16[256,128]{1,0:T(8,128)(2,1)S(1)} %bitcast.83), channel_id=1, source_target_pairs={{0,8},{8,16},{16,24},{24,32},{32,40},{40,48},{48,56},{56,64},{64,7... | collective-permute-start | bytes 196616 | tf_op jit(solution)/shard_map/ppermute | solution.py:16
  83.5 2.0 copy-start
  85.5 2.2 copy-start.1
  87.8 9.2 %collective-permute-start.4 = (bf16[256,128]{1,0:T(8,128)(2,1)S(1)}, bf16[256,128]{1,0:T(8,128)(2,1)S(1)}, u32[]{:S(2)}, u32[]{:S(2)}) collective-permute-start(bf16[256,128]{1,0:T(8,128)(2,1)S(1)} %get-tuple-element.7), channel_id=1, source_target_pairs={{0,8},{8,16},{16,24},{24,32},{32,40},{40,48},{48,56},{56,64},{64,7... | collective-permute-start | bytes 196616 | tf_op jit(solution)/shard_map/ppermute | solution.py:16
  89.7 9.1 %collective-permute-start.5 = (bf16[256,128]{1,0:T(8,128)(2,1)S(1)}, bf16[256,128]{1,0:T(8,128)(2,1)S(1)}, u32[]{:S(2)}, u32[]{:S(2)}) collective-permute-start(bf16[256,128]{1,0:T(8,128)(2,1)S(1)} %get-tuple-element.8), channel_id=1, source_target_pairs={{8,0},{16,8},{24,16},{32,24},{40,32},{48,40},{56,48},{64,56},{72,6... | collective-permute-start | bytes 196616 | tf_op jit(solution)/shard_map/ppermute | solution.py:19
  103.2 16.1 %collective-permute-start.6 = (bf16[256,128]{1,0:T(8,128)(2,1)S(1)}, bf16[256,128]{1,0:T(8,128)(2,1)S(1)}, u32[]{:S(2)}, u32[]{:S(2)}) collective-permute-start(bf16[256,128]{1,0:T(8,128)(2,1)S(1)} %get-tuple-element.5), channel_id=1, source_target_pairs={{0,8},{8,16},{16,24},{24,32},{32,40},{40,48},{48,56},{56,64},{64,7... | collective-permute-start | bytes 196616 | tf_op jit(solution)/shard_map/ppermute | solution.py:16
  105.1 14.1 %collective-permute-start.7 = (bf16[256,128]{1,0:T(8,128)(2,1)S(1)}, bf16[256,128]{1,0:T(8,128)(2,1)S(1)}, u32[]{:S(2)}, u32[]{:S(2)}) collective-permute-start(bf16[256,128]{1,0:T(8,128)(2,1)S(1)} %get-tuple-element.6), channel_id=1, source_target_pairs={{8,0},{16,8},{24,16},{32,24},{40,32},{48,40},{56,48},{64,56},{72,6... | collective-permute-start | bytes 196616 | tf_op jit(solution)/shard_map/ppermute | solution.py:19
  113.2 12.2 %all-to-all-start.1 = ((bf16[8,128,128]{2,1,0:T(8,128)(2,1)}), bf16[8,128,128]{2,1,0:T(8,128)(2,1)S(1)}, u32[]{:S(2)}, u32[]{:S(2)}) async-start(bf16[8,128,128]{2,1,0:T(8,128)(2,1)} %fusion.11), calls=%async_computation.1 | async-start | bytes 524288 | tf_op jit(solution)/shard_map/all_to_all | solution.py:49
  125.4 10.8 %all-to-all-start = ((bf16[8,128,128]{1,2,0:T(8,128)(2,1)}), bf16[8,128,128]{1,2,0:T(8,128)(2,1)S(1)}, u32[]{:S(2)}, u32[]{:S(2)}) async-start(bf16[8,128,128]{1,2,0:T(8,128)(2,1)} %fusion.8), calls=%async_computation | async-start | bytes 524288 | tf_op jit(solution)/shard_map/all_to_all | solution.py:50
  130.0 500.1 %all-reduce.2.cloned.1.call-start = ((), (), s32[]{:S(2)}) async-start(), calls=%async_computation.3 | async-start | bytes 8388608 | tf_op jit(solution)/shard_map/psum | solution.py:55
Sparse Core Ops, SparseCore 0:
  9.3 59.4 all-gather.1
  139.0 491.0 all-reduce.1
where the time goes:
time: 641 us; the launch traced here: 640 us
  waiting for transfers between devices  552 us (86%)
  starting transfers between devices  48.6 us (8%)
  matrix products  15.5 us (2%)
  between operations  13.6 us (2%)
  local copies, waits for them, and re-layouts  8.39 us (1%)
    psum x1, waiting for transfers between devices, body(): summed = lax.psum(partial_value, ('slab', 'band'))  491 us
    all_gather x1, waiting for transfers between devices, body(): full_tiles = lax.all_gather(hamiltonian, 'band', axis=2, tiled=True)  42.6 us
    ppermute x4, starting transfers between devices, padded(): lax.ppermute(lax.slice_in_dim(block, 0, width, axis=dim), axis, backward)  30.2 us
  transfers between devices with their start and end apart: 12, of which 7 were waited for; matrix products, arithmetic and copies ran while one was open for 2% of the time, Pallas kernels for 0%

commit v1 on v0

--- a/solution.py
+++ b/solution.py
@@ -33,7 +33,13 @@
 
 
 def body(hamiltonian, neighbors, orbitals):
-    full_tiles = lax.all_gather(hamiltonian, "band", axis=2, tiled=True)
+    convert_the_blocks = lambda in_array, d0: jnp.concatenate(
+        jax.lax.all_to_all(
+            jnp.stack([in_array for _ in range(jax.lax.axis_size("band"))]), "band", 0, 0
+        ),
+        axis=d0,
+    )
+    full_tiles = convert_the_blocks(hamiltonian, 2)
     first = apply_local(orbitals, full_tiles, neighbors).astype(jnp.bfloat16)
     second = (
         2.0 * apply_local(first, full_tiles, neighbors) - orbitals.astype(jnp.float32)

time: 641 us -> 615 us (0.959)
  waiting for transfers between devices: 552 us -> 510 us
  starting transfers between devices: 48.6 us -> 61.9 us
    all_gather x1 -> x0, waiting for transfers between devices: 42.6 us -> none  [body(): full_tiles = lax.all_gather(hamiltonian, 'band', axis=2, tiled=True)]
    all_to_all x0 -> x1, starting transfers between devices: none -> 10.2 us  [body(): jax.lax.all_to_all(jnp.stack([in_array for _ in range(jax.lax.axis_size('...]
  transfers between devices with their start and end apart: 12 -> 12, of which waited for: 7 -> 7; matrix products, arithmetic and copies ran while one was open for 2% -> 1% of each run, Pallas kernels for 0% -> 0%
where the time goes in v1:
time: 615 us; the launch traced here: 614 us
  waiting for transfers between devices  510 us (83%)
  starting transfers between devices  61.9 us (10%)
  matrix products  13.9 us (2%)
  between operations  13.6 us (2%)
  local copies, waits for them, and re-layouts  13.3 us (2%)
    psum x1, waiting for transfers between devices, body(): summed = lax.psum(partial_value, ('slab', 'band'))  487 us
    ppermute x4, starting transfers between devices, padded(): lax.ppermute(lax.slice_in_dim(block, 0, width, axis=dim), axis, backward)  33.5 us
  transfers between devices with their start and end apart: 12, of which 7 were waited for; matrix products, arithmetic and copies ran while one was open for 1% of the time, Pallas kernels for 0%

profile of v1, /device:TPU:2, one launch (start us, length us, event | category | flops | bytes accessed | tf_op | source)
XLA Modules:
  0.0 614.1 jit_solution(6813895752519994719)
XLA Ops:
  6.5 2.4 stack.2
  8.9 0.0 copy-start.1
  8.9 0.0 copy-start.2
  8.9 10.2 %all-to-all-start = ((bf16[8,8,7,16,128]{4,3,2,1,0:T(8,128)(2,1)}), bf16[8,8,7,16,128]{4,3,2,1,0:T(8,128)(2,1)}, u32[]{:S(2)}, u32[]{:S(2)}) async-start(bf16[8,8,7,16,128]{4,3,2,1,0:T(8,128)(2,1)} %stack.2), calls=%async_computation | async-start | bytes 3670016 | tf_op jit(solution)/shard_map/all_to_all | solution.py:37
  19.1 0.0 copy-done.1
  19.2 1.9 collective-permute-start
  21.1 7.7 %collective-permute-start.1 = (bf16[256,128]{1,0:T(8,128)(2,1)S(1)}, bf16[256,128]{1,0:T(8,128)(2,1)S(1)}, u32[]{:S(2)}, u32[]{:S(2)}) collective-permute-start(bf16[256,128]{1,0:T(8,128)(2,1)S(1)} %get-tuple-element.12), channel_id=1, source_target_pairs={{8,0},{16,8},{24,16},{32,24},{40,32},{48,40},{56,48},{64,56},{72,6... | collective-permute-start | bytes 196616 | tf_op jit(solution)/shard_map/ppermute | solution.py:19
  28.8 0.0 copy-done.2
  28.8 0.1 reshape.45
  28.9 0.0 collective-permute-done
  28.9 1.8 collective-permute-done.1
  30.7 2.1 gather_fusion
  32.8 5.3 all-to-all-done
  38.1 0.0 copy-start
  38.1 2.2 copy.8
  40.2 0.0 copy-done
  40.3 0.7 fusion.6
  40.9 11.3 %collective-permute-start.3 = (bf16[256,128]{1,0:T(8,128)(2,1)S(1)}, bf16[256,128]{1,0:T(8,128)(2,1)S(1)}, u32[]{:S(2)}, u32[]{:S(2)}) collective-permute-start(bf16[256,128]{1,0:T(8,128)(2,1)S(1)} %bitcast.90), channel_id=1, source_target_pairs={{8,0},{16,8},{24,16},{32,24},{40,32},{48,40},{56,48},{64,56},{72,6... | collective-permute-start | bytes 196616 | tf_op jit(solution)/shard_map/ppermute | solution.py:19
  52.2 1.9 collective-permute-start.2
  54.1 0.0 collective-permute-done.3
  54.2 7.3 %collective-permute-done.2 = bf16[256,128]{1,0:T(8,128)(2,1)S(1)} collective-permute-done((bf16[256,128]{1,0:T(8,128)(2,1)S(1)}, bf16[256,128]{1,0:T(8,128)(2,1)S(1)}, u32[]{:S(2)}, u32[]{:S(2)}) %collective-permute-start.2) | collective-permute-done | bytes 65568 | tf_op jit(solution)/shard_map/ppermute | solution.py:16
  61.4 2.1 gather_fusion.1
  63.5 2.1 fusion.3
  65.6 0.1 fusion.10
  65.7 1.9 collective-permute-start.4
  67.7 7.3 %collective-permute-start.5 = (bf16[256,128]{1,0:T(8,128)(2,1)S(1)}, bf16[256,128]{1,0:T(8,128)(2,1)S(1)}, u32[]{:S(2)}, u32[]{:S(2)}) collective-permute-start(bf16[256,128]{1,0:T(8,128)(2,1)S(1)} %get-tuple-element.8), channel_id=1, source_target_pairs={{8,0},{16,8},{24,16},{32,24},{40,32},{48,40},{56,48},{64,56},{72,6... | collective-permute-start | bytes 196616 | tf_op jit(solution)/shard_map/ppermute | solution.py:19
  74.9 0.0 collective-permute-done.4
  74.9 1.9 collective-permute-done.5
  76.8 2.1 gather_fusion.2
  78.9 2.1 fusion.4
  81.0 0.1 fusion.9
  81.1 1.9 collective-permute-start.6
  83.1 7.3 %collective-permute-start.7 = (bf16[256,128]{1,0:T(8,128)(2,1)S(1)}, bf16[256,128]{1,0:T(8,128)(2,1)S(1)}, u32[]{:S(2)}, u32[]{:S(2)}) collective-permute-start(bf16[256,128]{1,0:T(8,128)(2,1)S(1)} %get-tuple-element.6), channel_id=1, source_target_pairs={{8,0},{16,8},{24,16},{32,24},{40,32},{48,40},{56,48},{64,56},{72,6... | collective-permute-start | bytes 196616 | tf_op jit(solution)/shard_map/ppermute | solution.py:19
  90.4 0.8 fusion.11
  91.2 5.8 all-to-all-start.2
  97.0 0.0 collective-permute-done.6
  97.0 0.0 collective-permute-done.7
  97.0 2.1 gather_fusion.3
  99.1 3.0 fusion.8
  102.1 1.1 all-to-all-done.2
  103.1 4.7 all-to-all-start.1
  107.8 0.0 all-reduce.2.cloned.1.call-start
  107.8 0.2 copy.11
  108.0 5.9 all-to-all-done.1
  113.9 2.7 fusion.17
  116.6 0.0 all-reduce.2.cloned.1.call-update
  116.7 0.1 copy.10
  116.8 487.1 %all-reduce.2.cloned.1.call-done = f32[1024,1024]{1,0:T(8,128)} async-done(((f32[1024,1024]{1,0:T(8,128)}), f32[1024,1024]{1,0:T(8,128)}) %all-reduce.2.cloned.1.call-update) | async-done | bytes 4194320 | tf_op jit(solution)/shard_map/psum | solution.py:61
  603.9 3.4 fusion.7
  (10 shorter events, 0.2 us)
Async XLA Ops:
  8.9 10.2 %copy-start.1 = (bf16[1024,128]{1,0:T(8,128)(2,1)S(1)}, bf16[1024,128]{1,0:T(8,128)(2,1)}, u32[]{:S(2)}) copy-start(bf16[1024,128]{1,0:T(8,128)(2,1)} %param.5) | copy-start | bytes 786436
  8.9 19.9 %copy-start.2 = (s32[8,7]{1,0:T(8,128)S(1)}, s32[8,7]{1,0:T(8,128)}, u32[]{:S(2)}) copy-start(s32[8,7]{1,0:T(8,128)} %param.4) | copy-start | bytes 676
  8.9 29.1 %all-to-all-start = ((bf16[8,8,7,16,128]{4,3,2,1,0:T(8,128)(2,1)}), bf16[8,8,7,16,128]{4,3,2,1,0:T(8,128)(2,1)}, u32[]{:S(2)}, u32[]{:S(2)}) async-start(bf16[8,8,7,16,128]{4,3,2,1,0:T(8,128)(2,1)} %stack.2), calls=%async_computation | async-start | bytes 3670016 | tf_op jit(solution)/shard_map/all_to_all | solution.py:37
  19.2 9.8 %collective-permute-start = (bf16[256,128]{1,0:T(8,128)(2,1)S(1)}, bf16[256,128]{1,0:T(8,128)(2,1)S(1)}, u32[]{:S(2)}, u32[]{:S(2)}) collective-permute-start(bf16[256,128]{1,0:T(8,128)(2,1)S(1)} %get-tuple-element.11), channel_id=1, source_target_pairs={{0,8},{8,16},{16,24},{24,32},{32,40},{40,48},{48,56},{56,64},{64,7... | collective-permute-start | bytes 196616 | tf_op jit(solution)/shard_map/ppermute | solution.py:16
  21.1 9.6 %collective-permute-start.1 = (bf16[256,128]{1,0:T(8,128)(2,1)S(1)}, bf16[256,128]{1,0:T(8,128)(2,1)S(1)}, u32[]{:S(2)}, u32[]{:S(2)}) collective-permute-start(bf16[256,128]{1,0:T(8,128)(2,1)S(1)} %get-tuple-element.12), channel_id=1, source_target_pairs={{8,0},{16,8},{24,16},{32,24},{40,32},{48,40},{56,48},{64,56},{72,6... | collective-permute-start | bytes 196616 | tf_op jit(solution)/shard_map/ppermute | solution.py:19
  38.1 2.2 copy-start
  40.9 13.2 %collective-permute-start.3 = (bf16[256,128]{1,0:T(8,128)(2,1)S(1)}, bf16[256,128]{1,0:T(8,128)(2,1)S(1)}, u32[]{:S(2)}, u32[]{:S(2)}) collective-permute-start(bf16[256,128]{1,0:T(8,128)(2,1)S(1)} %bitcast.90), channel_id=1, source_target_pairs={{8,0},{16,8},{24,16},{32,24},{40,32},{48,40},{56,48},{64,56},{72,6... | collective-permute-start | bytes 196616 | tf_op jit(solution)/shard_map/ppermute | solution.py:19
  52.2 9.2 %collective-permute-start.2 = (bf16[256,128]{1,0:T(8,128)(2,1)S(1)}, bf16[256,128]{1,0:T(8,128)(2,1)S(1)}, u32[]{:S(2)}, u32[]{:S(2)}) collective-permute-start(bf16[256,128]{1,0:T(8,128)(2,1)S(1)} %bitcast.89), channel_id=1, source_target_pairs={{0,8},{8,16},{16,24},{24,32},{32,40},{40,48},{48,56},{56,64},{64,7... | collective-permute-start | bytes 196616 | tf_op jit(solution)/shard_map/ppermute | solution.py:16
  65.7 9.2 %collective-permute-start.4 = (bf16[256,128]{1,0:T(8,128)(2,1)S(1)}, bf16[256,128]{1,0:T(8,128)(2,1)S(1)}, u32[]{:S(2)}, u32[]{:S(2)}) collective-permute-start(bf16[256,128]{1,0:T(8,128)(2,1)S(1)} %get-tuple-element.7), channel_id=1, source_target_pairs={{0,8},{8,16},{16,24},{24,32},{32,40},{40,48},{48,56},{56,64},{64,7... | collective-permute-start | bytes 196616 | tf_op jit(solution)/shard_map/ppermute | solution.py:16
  67.7 9.1 %collective-permute-start.5 = (bf16[256,128]{1,0:T(8,128)(2,1)S(1)}, bf16[256,128]{1,0:T(8,128)(2,1)S(1)}, u32[]{:S(2)}, u32[]{:S(2)}) collective-permute-start(bf16[256,128]{1,0:T(8,128)(2,1)S(1)} %get-tuple-element.8), channel_id=1, source_target_pairs={{8,0},{16,8},{24,16},{32,24},{40,32},{48,40},{56,48},{64,56},{72,6... | collective-permute-start | bytes 196616 | tf_op jit(solution)/shard_map/ppermute | solution.py:19
  81.1 15.9 %collective-permute-start.6 = (bf16[256,128]{1,0:T(8,128)(2,1)S(1)}, bf16[256,128]{1,0:T(8,128)(2,1)S(1)}, u32[]{:S(2)}, u32[]{:S(2)}) collective-permute-start(bf16[256,128]{1,0:T(8,128)(2,1)S(1)} %get-tuple-element.5), channel_id=1, source_target_pairs={{0,8},{8,16},{16,24},{24,32},{32,40},{40,48},{48,56},{56,64},{64,7... | collective-permute-start | bytes 196616 | tf_op jit(solution)/shard_map/ppermute | solution.py:16
  83.1 13.9 %collective-permute-start.7 = (bf16[256,128]{1,0:T(8,128)(2,1)S(1)}, bf16[256,128]{1,0:T(8,128)(2,1)S(1)}, u32[]{:S(2)}, u32[]{:S(2)}) collective-permute-start(bf16[256,128]{1,0:T(8,128)(2,1)S(1)} %get-tuple-element.6), channel_id=1, source_target_pairs={{8,0},{16,8},{24,16},{32,24},{40,32},{48,40},{56,48},{64,56},{72,6... | collective-permute-start | bytes 196616 | tf_op jit(solution)/shard_map/ppermute | solution.py:19
  91.2 12.0 %all-to-all-start.2 = ((bf16[8,128,128]{2,1,0:T(8,128)(2,1)}), bf16[8,128,128]{2,1,0:T(8,128)(2,1)S(1)}, u32[]{:S(2)}, u32[]{:S(2)}) async-start(bf16[8,128,128]{2,1,0:T(8,128)(2,1)} %fusion.11), calls=%async_computation.2 | async-start | bytes 524288 | tf_op jit(solution)/shard_map/all_to_all | solution.py:55
  103.1 10.8 %all-to-all-start.1 = ((bf16[8,128,128]{1,2,0:T(8,128)(2,1)}), bf16[8,128,128]{1,2,0:T(8,128)(2,1)S(1)}, u32[]{:S(2)}, u32[]{:S(2)}) async-start(bf16[8,128,128]{1,2,0:T(8,128)(2,1)} %fusion.8), calls=%async_computation.1 | async-start | bytes 524288 | tf_op jit(solution)/shard_map/all_to_all | solution.py:56
  107.8 496.0 %all-reduce.2.cloned.1.call-start = ((), (), s32[]{:S(2)}) async-start(), calls=%async_computation.3 | async-start | bytes 8388608 | tf_op jit(solution)/shard_map/psum | solution.py:61
Sparse Core Ops, SparseCore 0:
  116.8 487.0 all-reduce.1
